TPU v7x, 256 devices: a whole 4x4x8 slice. The times are simulated.
256 devices in a mesh: corner: 16 (over y, x_lo, core), tm: 16 (over z, x_hi).
Axes of the slice: x: 4 (x_hi: 2, x_lo: 2; x = x_hi * 2 + x_lo), y: 4, z: 8, core: 2. Of those that a mesh axis runs over, the one named last changes fastest.
Arguments:
- signal: bfloat16 [16, 64, 65536], P('corner', None, 'tm'), may hold values from -6 to 6
- dilated_conv_weight: bfloat16 [2, 256, 128], replicated, may hold values from -0.5 to 0.5
- dilated_conv_bias: float32 [2, 256], replicated, may hold values from -3 to 3
- projection_weight: bfloat16 [2, 128, 128], replicated, may hold values from -0.5 to 0.5
- projection_bias: float32 [2, 128], replicated, may hold values from -3 to 3
- cot_top: bfloat16 [16, 64, 65536], P('corner', None, 'tm'), may hold values from -6 to 6
- cot_skip: bfloat16 [16, 64, 65536], P('corner', None, 'tm'), may hold values from -6 to 6
Outputs:
- x_top: bfloat16 [16, 64, 65536], P('corner', None, 'tm')
- skip_sum: bfloat16 [16, 64, 65536], P('corner', None, 'tm')
- grad_input: bfloat16 [16, 64, 65536], P('corner', None, 'tm')
- grad_conv: float32 [2, 256, 128], replicated
- grad_conv_bias: float32 [2, 256], replicated
- grad_out: float32 [2, 128, 128], replicated
- grad_out_bias: float32 [2, 128], replicated
All inputs are finite; a program needn't handle non-finite values.
Results may differ from a plain program's by a relative error of at most 0.0065.
Values may be sent and summed in bfloat16 or wider, within the bound.
No kernel may reach another device: no remote copies, remote signals or barrier semaphores. Data moves between devices by JAX's collectives and lax.ppermute only.
A program may use at most 64 MiB of HBM per device.

v0:
```python
import math
import jax
import jax.numpy as jnp
from jax import lax
from jax.sharding import PartitionSpec as P


def from_behind(block, axis, distance):
    devices = range(lax.axis_size(axis))
    route = [(i - distance, i) for i in devices if i - distance in devices]
    return lax.ppermute(block, axis, route)


def gated_layer_forward(a_in, tap_in, weight, bias, proj, proj_bias, gsize, rsize):
    stacked = jnp.concatenate([tap_in, a_in], axis=1)
    pre_act = (
        jnp.einsum("oc,bct->bot", weight, stacked, preferred_element_type=jnp.float32)
        + bias[None, :, None]
    )
    gate_out = (jnp.tanh(pre_act[:, :gsize]) * jax.nn.sigmoid(pre_act[:, gsize:])).astype(
        jnp.bfloat16
    )
    mixed = (
        jnp.einsum("og,bgt->bot", proj, gate_out, preferred_element_type=jnp.float32)
        + proj_bias[None, :, None]
    )
    next_act = (a_in.astype(jnp.float32) + mixed[:, :rsize]).astype(jnp.bfloat16)
    return (stacked, pre_act, gate_out, next_act, mixed[:, rsize:])


def layer_backward(go_res, go_skip, stacked, pre_act, gate_out, weight, proj, gsize, rsize):
    upper = jnp.concatenate([go_res, go_skip], axis=1)
    grad_proj = jnp.einsum("bot,bgt->og", upper, gate_out, preferred_element_type=jnp.float32)
    grad_pbias = jnp.sum(upper, axis=(0, 2), dtype=jnp.float32)
    grad_gate = jnp.einsum("og,bot->bgt", proj, upper, preferred_element_type=jnp.float32)
    filt_act = jnp.tanh(pre_act[:, :gsize])
    gate_act = jax.nn.sigmoid(pre_act[:, gsize:])
    grad_pre = jnp.concatenate(
        [
            grad_gate * gate_act * (1.0 - filt_act * filt_act),
            grad_gate * filt_act * gate_act * (1.0 - gate_act),
        ],
        axis=1,
    ).astype(jnp.bfloat16)
    grad_weight = jnp.einsum("bot,bct->oc", grad_pre, stacked, preferred_element_type=jnp.float32)
    grad_bias = jnp.sum(grad_pre, axis=(0, 2), dtype=jnp.float32)
    grad_in = jnp.einsum("oc,bot->bct", weight, grad_pre, preferred_element_type=jnp.float32)
    return (
        grad_in[:, :rsize].astype(jnp.bfloat16),
        grad_in[:, rsize:],
        (grad_weight, grad_bias, grad_proj, grad_pbias),
    )


def on_device(
    signal,
    dilated_conv_weight,
    dilated_conv_bias,
    projection_weight,
    projection_bias,
    cot_top,
    cot_skip,
):
    rsize = signal.shape[1]
    gsize = projection_weight.shape[2]
    tap_near = from_behind(signal, "tm", 1)
    (
        lower_saved_state,
        lower_preactivation,
        lower_gated_output,
        middle_layer_input,
        lower_skip_output,
    ) = gated_layer_forward(
        signal,
        tap_near,
        dilated_conv_weight[0],
        dilated_conv_bias[0],
        projection_weight[0],
        projection_bias[0],
        gsize,
        rsize,
    )
    tap_far = from_behind(middle_layer_input, "tm", 2)
    (
        upper_saved_state,
        upper_preactivation,
        upper_gated_output,
        upper_layer_output,
        upper_skip_output,
    ) = gated_layer_forward(
        middle_layer_input,
        tap_far,
        dilated_conv_weight[1],
        dilated_conv_bias[1],
        projection_weight[1],
        projection_bias[1],
        gsize,
        rsize,
    )
    skip_out = (lower_skip_output + upper_skip_output).astype(jnp.bfloat16)
    delayed_gradient_upper, current_gradient_upper, grads_top = layer_backward(
        cot_top,
        cot_skip,
        upper_saved_state,
        upper_preactivation,
        upper_gated_output,
        dilated_conv_weight[1],
        projection_weight[1],
        gsize,
        rsize,
    )
    later_top = from_behind(delayed_gradient_upper, "tm", -2)
    middle_input_gradient = (
        cot_top.astype(jnp.float32) + current_gradient_upper + later_top.astype(jnp.float32)
    ).astype(jnp.bfloat16)
    delayed_gradient_lower, current_gradient_lower, grads_low = layer_backward(
        middle_input_gradient,
        cot_skip,
        lower_saved_state,
        lower_preactivation,
        lower_gated_output,
        dilated_conv_weight[0],
        projection_weight[0],
        gsize,
        rsize,
    )
    later_low = from_behind(delayed_gradient_lower, "tm", -1)
    lower_input_gradient = (
        middle_input_gradient.astype(jnp.float32)
        + current_gradient_lower
        + later_low.astype(jnp.float32)
    ).astype(jnp.bfloat16)
    summed = lax.psum(
        (
            jnp.stack([grads_low[0], grads_top[0]]),
            jnp.stack([grads_low[1], grads_top[1]]),
            jnp.stack([grads_low[2], grads_top[2]]),
            jnp.stack([grads_low[3], grads_top[3]]),
        ),
        ("corner", "tm"),
    )
    count = signal.shape[0] * lax.axis_size("corner") * signal.shape[2] * lax.axis_size("tm")
    scale = 1.0 / math.sqrt(count)
    return (
        upper_layer_output,
        skip_out,
        lower_input_gradient,
        summed[0] * scale,
        summed[1] * scale,
        summed[2] * scale,
        summed[3] * scale,
    )


def solution(mesh):
    return jax.shard_map(
        on_device,
        mesh=mesh,
        in_specs=(
            P("corner", None, "tm"),
            P(),
            P(),
            P(),
            P(),
            P("corner", None, "tm"),
            P("corner", None, "tm"),
        ),
        out_specs=(
            P("corner", None, "tm"),
            P("corner", None, "tm"),
            P("corner", None, "tm"),
            P(),
            P(),
            P(),
            P(),
        ),
        check_vma=False,
    )
```

profile of v0, /device:TPU:1, one launch (start us, length us, event | category | flops | bytes accessed | tf_op | source)
XLA Modules:
  0.0 411.1 jit_solution(4979422311224916654)
XLA Ops:
  7.2 5.5 %collective-permute-start = (bf16[1,64,4096]{2,1,0:T(8,128)(2,1)}, bf16[1,64,4096]{2,1,0:T(8,128)(2,1)S(1)}, u32[]{:S(2)}, u32[]{:S(2)}) collective-permute-start(bf16[1,64,4096]{2,1,0:T(8,128)(2,1)} %param.7), channel_id=1, source_target_pairs={{0,1},{1,2},{2,3},{3,4},{4,5},{5,6},{6,7},{7,8},{8,9},{9,10},{10,1... | collective-permute-start | bytes 1572872 | tf_op jit(solution)/shard_map/ppermute | solution.py:11
  12.7 0.8 fusion.55
  13.5 0.8 slice_bitcast_fusion
  14.2 1.1 constant_dynamic-update-slice_fusion.1
  15.3 8.3 %collective-permute-done = bf16[1,64,4096]{2,1,0:T(8,128)(2,1)S(1)} collective-permute-done((bf16[1,64,4096]{2,1,0:T(8,128)(2,1)}, bf16[1,64,4096]{2,1,0:T(8,128)(2,1)S(1)}, u32[]{:S(2)}, u32[]{:S(2)}) %collective-permute-start) | collective-permute-done | bytes 524320 | tf_op jit(solution)/shard_map/ppermute | solution.py:11
  23.6 2.0 fusion.1
  25.6 0.8 fusion.18
  26.9 0.6 copy-done.6
  27.6 5.3 %collective-permute-start.1 = (bf16[1,64,4096]{2,1,0:T(8,128)(2,1)S(1)}, bf16[1,64,4096]{2,1,0:T(8,128)(2,1)S(1)}, u32[]{:S(2)}, u32[]{:S(2)}) collective-permute-start(bf16[1,64,4096]{2,1,0:T(8,128)(2,1)S(1)} %fusion.26), channel_id=1, source_target_pairs={{0,2},{1,3},{2,4},{3,5},{4,6},{5,7},{6,8},{7,9},{8,10},{9,11},{10,... | collective-permute-start | bytes 1572872 | tf_op jit(solution)/shard_map/ppermute | solution.py:11
  33.2 9.3 %collective-permute-done.1 = bf16[1,64,4096]{2,1,0:T(8,128)(2,1)S(1)} collective-permute-done((bf16[1,64,4096]{2,1,0:T(8,128)(2,1)S(1)}, bf16[1,64,4096]{2,1,0:T(8,128)(2,1)S(1)}, u32[]{:S(2)}, u32[]{:S(2)}) %collective-permute-start.1) | collective-permute-done | bytes 524320 | tf_op jit(solution)/shard_map/ppermute | solution.py:11
  42.5 0.7 fusion.3
  43.3 1.5 multiply_convert_fusion.3
  44.8 0.5 convolution_bitcast_fusion.6
  45.3 1.3 collective-permute-start.2
  47.0 1.2 fusion.24
  48.6 0.7 fusion.16
  49.3 0.4 convolution_bitcast_fusion.8
  49.8 9.4 %collective-permute-done.2 = bf16[1,64,4096]{2,1,0:T(8,128)(2,1)S(1)} collective-permute-done((bf16[1,64,4096]{2,1,0:T(8,128)(2,1)S(1)}, bf16[1,64,4096]{2,1,0:T(8,128)(2,1)S(1)}, u32[]{:S(2)}, u32[]{:S(2)}) %collective-permute-start.2) | collective-permute-done | bytes 524320 | tf_op jit(solution)/shard_map/ppermute | solution.py:11
  59.3 1.3 multiply_convert_fusion.1
  62.0 82.7 %all-reduce = (f32[2,256]{1,0:T(2,128)S(1)}, f32[2,128]{1,0:T(2,128)S(1)}) all-reduce(f32[2,256]{1,0:T(2,128)S(1)} %pad_maximum_fusion.15, f32[2,128]{1,0:T(2,128)S(1)} %pad_maximum_fusion.16), channel_id=1, replica_groups=mesh['corner'=16,'tm'=16] {'corner','tm'}, use_global_device_ids=true, to_apply=%region_3.0 | all-reduce | flops 768 | bytes 6144 | tf_op jit(solution)/shard_map/psum | solution.py:133
  144.7 0.6 broadcast_multiply_fusion.2
  145.3 2.2 convolution_bitcast_fusion.4
  147.5 0.8 slice.202
  148.3 1.3 collective-permute-start.3
  149.6 0.7 pad_maximum_fusion.14
  150.3 0.7 fusion.17
  151.0 0.7 pad_maximum_fusion.13
  151.7 0.6 broadcast_multiply_fusion.3
  152.3 246.7 %all-reduce.4.cloned.1.call-done = (f32[2,256,128]{2,1,0:T(8,128)}, f32[2,128,128]{2,1,0:T(8,128)}) async-done(((f32[2,256,128]{2,1,0:T(8,128)}, f32[2,128,128]{2,1,0:T(8,128)}), (f32[2,256,128]{2,1,0:T(8,128)}, f32[2,128,128]{2,1,0:T(8,128)})) %all-reduce.4.cloned.1.call-update) | async-done | bytes 393232 | tf_op jit(solution)/shard_map/psum | solution.py:133
  399.0 1.6 broadcast_multiply_fusion.1
  400.6 1.7 broadcast_multiply_fusion
  402.2 2.0 fusion.21
  (37 shorter events, 3.2 us)
Async XLA Ops:
  7.2 391.8 %all-reduce.4.cloned.1.call-start = ((), (), s32[]{:S(2)}) async-start(), calls=%async_computation | async-start | bytes 786432 | tf_op jit(solution)/shard_map/psum | solution.py:133
  7.2 16.4 %collective-permute-start = (bf16[1,64,4096]{2,1,0:T(8,128)(2,1)}, bf16[1,64,4096]{2,1,0:T(8,128)(2,1)S(1)}, u32[]{:S(2)}, u32[]{:S(2)}) collective-permute-start(bf16[1,64,4096]{2,1,0:T(8,128)(2,1)} %param.7), channel_id=1, source_target_pairs={{0,1},{1,2},{2,3},{3,4},{4,5},{5,6},{6,7},{7,8},{8,9},{9,10},{10,1... | collective-permute-start | bytes 1572872 | tf_op jit(solution)/shard_map/ppermute | solution.py:11
  23.6 2.0 copy-start.8
  25.6 0.9 copy-start.10
  26.4 1.0 copy-start.6
  26.4 6.5 %copy-start.5 = (bf16[1,64,4096]{2,1,0:T(8,128)(2,1)S(1)}, bf16[1,64,4096]{2,1,0:T(8,128)(2,1)}, u32[]{:S(2)}) copy-start(bf16[1,64,4096]{2,1,0:T(8,128)(2,1)} %param.13) | copy-start | bytes 1572868
  27.5 15.1 %copy-start.7 = (bf16[2,256,128]{2,1,0:T(8,128)(2,1)S(1)}, bf16[2,256,128]{2,1,0:T(8,128)(2,1)}, u32[]{:S(2)}) copy-start(bf16[2,256,128]{2,1,0:T(8,128)(2,1)} %param.8) | copy-start | bytes 393220
  27.6 15.0 %collective-permute-start.1 = (bf16[1,64,4096]{2,1,0:T(8,128)(2,1)S(1)}, bf16[1,64,4096]{2,1,0:T(8,128)(2,1)S(1)}, u32[]{:S(2)}, u32[]{:S(2)}) collective-permute-start(bf16[1,64,4096]{2,1,0:T(8,128)(2,1)S(1)} %fusion.26), channel_id=1, source_target_pairs={{0,2},{1,3},{2,4},{3,5},{4,6},{5,7},{6,8},{7,9},{8,10},{9,11},{10,... | collective-permute-start | bytes 1572872 | tf_op jit(solution)/shard_map/ppermute | solution.py:11
  45.3 13.9 %collective-permute-start.2 = (bf16[1,64,4096]{2,1,0:T(8,128)(2,1)S(1)}, bf16[1,64,4096]{2,1,0:T(8,128)(2,1)S(1)}, u32[]{:S(2)}, u32[]{:S(2)}) collective-permute-start(bf16[1,64,4096]{2,1,0:T(8,128)(2,1)S(1)} %slice.203), channel_id=1, source_target_pairs={{2,0},{3,1},{4,2},{5,3},{6,4},{7,5},{8,6},{9,7},{10,8},{11,9},{12,... | collective-permute-start | bytes 1572872 | tf_op jit(solution)/shard_map/ppermute | solution.py:11
  49.3 9.8 %copy-start.4 = (bf16[1,64,4096]{2,1,0:T(8,128)(2,1)S(1)}, bf16[1,64,4096]{2,1,0:T(8,128)(2,1)}, u32[]{:S(2)}) copy-start(bf16[1,64,4096]{2,1,0:T(8,128)(2,1)} %param.12) | copy-start | bytes 1572868
  60.7 1.1 copy-start
  60.7 1.3 copy-start.2
  145.3 5.0 %copy-start.1 = (bf16[1,128,4096]{2,1,0:T(8,128)(2,1)S(1)}, bf16[1,128,4096]{2,1,0:T(8,128)(2,1)}, u32[]{:S(2)}) copy-start(bf16[1,128,4096]{2,1,0:T(8,128)(2,1)} %copy-done) | copy-start | bytes 3145732
  145.3 5.0 %copy-start.3 = (bf16[1,128,4096]{2,1,0:T(8,128)(2,1)S(1)}, bf16[1,128,4096]{2,1,0:T(8,128)(2,1)}, u32[]{:S(2)}) copy-start(bf16[1,128,4096]{2,1,0:T(8,128)(2,1)} %copy-done.2) | copy-start | bytes 3145732
  145.3 5.0 %copy-start.9 = (bf16[1,64,4096]{2,1,0:T(8,128)(2,1)S(1)}, bf16[1,64,4096]{2,1,0:T(8,128)(2,1)}, u32[]{:S(2)}) copy-start(bf16[1,64,4096]{2,1,0:T(8,128)(2,1)} %copy-done.8) | copy-start | bytes 1572868
  148.3 253.9 %collective-permute-start.3 = (bf16[1,64,4096]{2,1,0:T(8,128)(2,1)}, bf16[1,64,4096]{2,1,0:T(8,128)(2,1)}, u32[]{:S(2)}, u32[]{:S(2)}) collective-permute-start(bf16[1,64,4096]{2,1,0:T(8,128)(2,1)} %slice.202), channel_id=1, source_target_pairs={{1,0},{2,1},{3,2},{4,3},{5,4},{6,5},{7,6},{8,7},{9,8},{10,9},{11,1... | collective-permute-start | bytes 1572872 | tf_op jit(solution)/shard_map/ppermute | solution.py:11
Sparse Core Ops, SparseCore 0:
  151.9 247.0 all-reduce.3
where the time goes:
time: 412 us; the launch traced here: 411 us
  waiting for transfers between devices  274 us (67%)
  blocking collectives  82.7 us (20%)
  between operations  14.3 us (3%)
  starting transfers between devices  13.5 us (3%)
  matrix products  11.3 us (3%)
  other arithmetic  11.3 us (3%)
  local copies, waits for them, and re-layouts  4.41 us (1%)
    psum x1, waiting for transfers between devices, on_device(): lax.psum((jnp.stack([grads_low[0], grads_top[0]]), jnp.stack([grads_low[1...  247 us
    psum x1, blocking collectives, on_device(): lax.psum((jnp.stack([grads_low[0], grads_top[0]]), jnp.stack([grads_low[1...  82.7 us
    ppermute x4, waiting for transfers between devices, from_behind(): return lax.ppermute(block, axis, route)  27 us
    ppermute x4, starting transfers between devices, from_behind(): return lax.ppermute(block, axis, route)  13.4 us
  transfers between devices with their start and end apart: 5, of which 4 were waited for; matrix products, arithmetic and copies ran while one was open for 3% of the time, Pallas kernels for 0%

commit v1 on v0

--- a/solution.py
+++ b/solution.py
@@ -130,15 +130,14 @@
         + current_gradient_lower
         + later_low.astype(jnp.float32)
     ).astype(jnp.bfloat16)
-    summed = lax.psum(
-        (
-            jnp.stack([grads_low[0], grads_top[0]]),
-            jnp.stack([grads_low[1], grads_top[1]]),
-            jnp.stack([grads_low[2], grads_top[2]]),
-            jnp.stack([grads_low[3], grads_top[3]]),
-        ),
-        ("corner", "tm"),
+    summed = (
+        jnp.stack([grads_low[0], grads_top[0]]),
+        jnp.stack([grads_low[1], grads_top[1]]),
+        jnp.stack([grads_low[2], grads_top[2]]),
+        jnp.stack([grads_low[3], grads_top[3]]),
     )
+    for it in ("tm", "corner"):
+        summed = lax.psum(summed, axis_name=it)
     count = signal.shape[0] * lax.axis_size("corner") * signal.shape[2] * lax.axis_size("tm")
     scale = 1.0 / math.sqrt(count)
     return (

time: 412 us -> 368 us (0.89)
  waiting for transfers between devices: 274 us -> 240 us
  blocking collectives: 82.7 us -> 75.9 us
    psum x1 -> x2, waiting for transfers between devices: 247 us -> 213 us  [on_device(): summed = lax.psum(summed, axis_name=it)]
    psum x1 -> x2, blocking collectives: 82.7 us -> 75.9 us  [on_device(): summed = lax.psum(summed, axis_name=it)]
  transfers between devices with their start and end apart: 5 -> 6, of which waited for: 4 -> 5; matrix products, arithmetic and copies ran while one was open for 3% -> 3% of each run, Pallas kernels for 0% -> 0%
where the time goes in v1:
time: 368 us; the launch traced here: 367 us
  waiting for transfers between devices  240 us (65%)
  blocking collectives  75.9 us (21%)
  between operations  14.3 us (4%)
  starting transfers between devices  13.5 us (4%)
  other arithmetic  10.2 us (3%)
  matrix products  9.4 us (3%)
  local copies, waits for them, and re-layouts  4.14 us (1%)
    psum x2, waiting for transfers between devices, on_device(): summed = lax.psum(summed, axis_name=it)  213 us
    psum x2, blocking collectives, on_device(): summed = lax.psum(summed, axis_name=it)  75.9 us
    ppermute x4, waiting for transfers between devices, from_behind(): return lax.ppermute(block, axis, route)  27 us
    ppermute x4, starting transfers between devices, from_behind(): return lax.ppermute(block, axis, route)  13.4 us
  transfers between devices with their start and end apart: 6, of which 5 were waited for; matrix products, arithmetic and copies ran while one was open for 3% of the time, Pallas kernels for 0%

profile of v1, /device:TPU:1, one launch (start us, length us, event | category | flops | bytes accessed | tf_op | source)
XLA Modules:
  0.0 367.5 jit_solution(3252384787430136955)
XLA Ops:
  7.2 5.5 %collective-permute-start = (bf16[1,64,4096]{2,1,0:T(8,128)(2,1)}, bf16[1,64,4096]{2,1,0:T(8,128)(2,1)S(1)}, u32[]{:S(2)}, u32[]{:S(2)}) collective-permute-start(bf16[1,64,4096]{2,1,0:T(8,128)(2,1)} %param.7), channel_id=1, source_target_pairs={{0,1},{1,2},{2,3},{3,4},{4,5},{5,6},{6,7},{7,8},{8,9},{9,10},{10,1... | collective-permute-start | bytes 1572872 | tf_op jit(solution)/shard_map/ppermute | solution.py:11
  12.7 0.8 fusion.55
  13.5 0.8 slice_bitcast_fusion
  14.2 1.1 constant_dynamic-update-slice_fusion.1
  15.3 8.3 %collective-permute-done = bf16[1,64,4096]{2,1,0:T(8,128)(2,1)S(1)} collective-permute-done((bf16[1,64,4096]{2,1,0:T(8,128)(2,1)}, bf16[1,64,4096]{2,1,0:T(8,128)(2,1)S(1)}, u32[]{:S(2)}, u32[]{:S(2)}) %collective-permute-start) | collective-permute-done | bytes 524320 | tf_op jit(solution)/shard_map/ppermute | solution.py:11
  23.6 1.8 fusion.1
  25.4 0.8 fusion.18
  26.7 0.6 copy-done.2
  27.4 5.3 %collective-permute-start.1 = (bf16[1,64,4096]{2,1,0:T(8,128)(2,1)S(1)}, bf16[1,64,4096]{2,1,0:T(8,128)(2,1)S(1)}, u32[]{:S(2)}, u32[]{:S(2)}) collective-permute-start(bf16[1,64,4096]{2,1,0:T(8,128)(2,1)S(1)} %fusion.26), channel_id=1, source_target_pairs={{0,2},{1,3},{2,4},{3,5},{4,6},{5,7},{6,8},{7,9},{8,10},{9,11},{10,... | collective-permute-start | bytes 1572872 | tf_op jit(solution)/shard_map/ppermute | solution.py:11
  33.0 9.3 %collective-permute-done.1 = bf16[1,64,4096]{2,1,0:T(8,128)(2,1)S(1)} collective-permute-done((bf16[1,64,4096]{2,1,0:T(8,128)(2,1)S(1)}, bf16[1,64,4096]{2,1,0:T(8,128)(2,1)S(1)}, u32[]{:S(2)}, u32[]{:S(2)}) %collective-permute-start.1) | collective-permute-done | bytes 524320 | tf_op jit(solution)/shard_map/ppermute | solution.py:11
  42.3 0.7 fusion.3
  43.0 1.5 multiply_convert_fusion.3
  45.1 1.3 collective-permute-start.2
  46.8 1.2 fusion.24
  48.3 0.7 fusion.16
  49.5 9.4 %collective-permute-done.2 = bf16[1,64,4096]{2,1,0:T(8,128)(2,1)S(1)} collective-permute-done((bf16[1,64,4096]{2,1,0:T(8,128)(2,1)S(1)}, bf16[1,64,4096]{2,1,0:T(8,128)(2,1)S(1)}, u32[]{:S(2)}, u32[]{:S(2)}) %collective-permute-start.2) | collective-permute-done | bytes 524320 | tf_op jit(solution)/shard_map/ppermute | solution.py:11
  59.1 1.3 multiply_convert_fusion.1
  61.5 0.5 convolution_bitcast_fusion.4
  62.0 0.8 slice.202
  62.8 1.3 collective-permute-start.3
  64.1 0.7 pad_maximum_fusion.14
  64.8 0.7 fusion.17
  65.5 0.7 pad_maximum_fusion.13
  66.3 39.2 %all-reduce = (f32[2,256]{1,0:T(2,128)S(1)}, f32[2,128]{1,0:T(2,128)S(1)}) all-reduce(f32[2,256]{1,0:T(2,128)S(1)} %pad_maximum_fusion.15, f32[2,128]{1,0:T(2,128)S(1)} %pad_maximum_fusion.16), channel_id=1, replica_groups=mesh['corner'=16,'tm'=16] {'tm'}, use_global_device_ids=true, to_apply=%region_4.0 | all-reduce | flops 768 | bytes 6144 | tf_op jit(solution)/shard_map/psum | solution.py:140
  105.5 36.7 %all-reduce.2 = (f32[2,256]{1,0:T(2,128)S(1)}, f32[2,128]{1,0:T(2,128)S(1)}) all-reduce(f32[2,256]{1,0:T(2,128)S(1)} %get-tuple-element.7, f32[2,128]{1,0:T(2,128)S(1)} %get-tuple-element.8), channel_id=1, replica_groups=mesh['corner'=16,'tm'=16] {'corner'}, use_global_device_ids=true, to_apply=%region_5.0 | all-reduce | flops 768 | bytes 6144 | tf_op jit(solution)/shard_map/psum | solution.py:140
  142.2 0.6 broadcast_multiply_fusion.3
  142.8 0.6 broadcast_multiply_fusion.2
  143.4 80.3 %all-reduce.7.cloned.1.call-done = (f32[2,256,128]{2,1,0:T(8,128)}, f32[2,128,128]{2,1,0:T(8,128)}) async-done(((f32[2,256,128]{2,1,0:T(8,128)}, f32[2,128,128]{2,1,0:T(8,128)}), (f32[2,256,128]{2,1,0:T(8,128)}, f32[2,128,128]{2,1,0:T(8,128)})) %all-reduce.7.cloned.1.call-update) | async-done | bytes 393232 | tf_op jit(solution)/shard_map/psum | solution.py:140
  223.7 1.0 fusion.21
  224.7 132.7 %all-reduce.9.cloned.1.call-done = (f32[2,256,128]{2,1,0:T(8,128)}, f32[2,128,128]{2,1,0:T(8,128)}) async-done(((f32[2,256,128]{2,1,0:T(8,128)}, f32[2,128,128]{2,1,0:T(8,128)}), (f32[2,256,128]{2,1,0:T(8,128)}, f32[2,128,128]{2,1,0:T(8,128)})) %all-reduce.9.cloned.1.call-update) | async-done | bytes 393232 | tf_op jit(solution)/shard_map/psum | solution.py:140
  357.4 1.7 broadcast_multiply_fusion
  359.1 1.6 broadcast_multiply_fusion.1
  (29 shorter events, 3.9 us)
Async XLA Ops:
  7.2 216.5 %all-reduce.7.cloned.1.call-start = ((), (), s32[]{:S(2)}) async-start(), calls=%async_computation | async-start | bytes 786432 | tf_op jit(solution)/shard_map/psum | solution.py:140
  7.2 16.4 %collective-permute-start = (bf16[1,64,4096]{2,1,0:T(8,128)(2,1)}, bf16[1,64,4096]{2,1,0:T(8,128)(2,1)S(1)}, u32[]{:S(2)}, u32[]{:S(2)}) collective-permute-start(bf16[1,64,4096]{2,1,0:T(8,128)(2,1)} %param.7), channel_id=1, source_target_pairs={{0,1},{1,2},{2,3},{3,4},{4,5},{5,6},{6,7},{7,8},{8,9},{9,10},{10,1... | collective-permute-start | bytes 1572872 | tf_op jit(solution)/shard_map/ppermute | solution.py:11
  25.4 0.9 copy-start.4
  26.2 1.0 copy-start.2
  26.2 6.5 %copy-start.1 = (bf16[1,64,4096]{2,1,0:T(8,128)(2,1)S(1)}, bf16[1,64,4096]{2,1,0:T(8,128)(2,1)}, u32[]{:S(2)}) copy-start(bf16[1,64,4096]{2,1,0:T(8,128)(2,1)} %param.13) | copy-start | bytes 1572868
  27.3 15.1 %copy-start.3 = (bf16[2,256,128]{2,1,0:T(8,128)(2,1)S(1)}, bf16[2,256,128]{2,1,0:T(8,128)(2,1)}, u32[]{:S(2)}) copy-start(bf16[2,256,128]{2,1,0:T(8,128)(2,1)} %param.8) | copy-start | bytes 393220
  27.4 15.0 %collective-permute-start.1 = (bf16[1,64,4096]{2,1,0:T(8,128)(2,1)S(1)}, bf16[1,64,4096]{2,1,0:T(8,128)(2,1)S(1)}, u32[]{:S(2)}, u32[]{:S(2)}) collective-permute-start(bf16[1,64,4096]{2,1,0:T(8,128)(2,1)S(1)} %fusion.26), channel_id=1, source_target_pairs={{0,2},{1,3},{2,4},{3,5},{4,6},{5,7},{6,8},{7,9},{8,10},{9,11},{10,... | collective-permute-start | bytes 1572872 | tf_op jit(solution)/shard_map/ppermute | solution.py:11
  45.1 13.9 %collective-permute-start.2 = (bf16[1,64,4096]{2,1,0:T(8,128)(2,1)S(1)}, bf16[1,64,4096]{2,1,0:T(8,128)(2,1)S(1)}, u32[]{:S(2)}, u32[]{:S(2)}) collective-permute-start(bf16[1,64,4096]{2,1,0:T(8,128)(2,1)S(1)} %slice.203), channel_id=1, source_target_pairs={{2,0},{3,1},{4,2},{5,3},{6,4},{7,5},{8,6},{9,7},{10,8},{11,9},{12,... | collective-permute-start | bytes 1572872 | tf_op jit(solution)/shard_map/ppermute | solution.py:11
  49.0 9.9 %copy-start = (bf16[1,64,4096]{2,1,0:T(8,128)(2,1)S(1)}, bf16[1,64,4096]{2,1,0:T(8,128)(2,1)}, u32[]{:S(2)}) copy-start(bf16[1,64,4096]{2,1,0:T(8,128)(2,1)} %param.12) | copy-start | bytes 1572868
  62.8 160.9 %collective-permute-start.3 = (bf16[1,64,4096]{2,1,0:T(8,128)(2,1)}, bf16[1,64,4096]{2,1,0:T(8,128)(2,1)S(1)}, u32[]{:S(2)}, u32[]{:S(2)}) collective-permute-start(bf16[1,64,4096]{2,1,0:T(8,128)(2,1)} %slice.202), channel_id=1, source_target_pairs={{1,0},{2,1},{3,2},{4,3},{5,4},{6,5},{7,6},{8,7},{9,8},{10,9},{11,1... | collective-permute-start | bytes 1572872 | tf_op jit(solution)/shard_map/ppermute | solution.py:11
  66.3 291.1 %all-reduce.9.cloned.1.call-start = ((), (), s32[]{:S(2)}) async-start(), calls=%async_computation.1 | async-start | bytes 786432 | tf_op jit(solution)/shard_map/psum | solution.py:140
Sparse Core Ops, SparseCore 0:
  66.4 157.2 all-reduce.6
  226.5 130.8 all-reduce.8
